TPU v7x, 32 devices: a whole 2x2x4 slice. The times are simulated.
32 devices in a mesh: freq: 8 (over z, x), pol: 2 (over core), beam: 2 (over y).
Axes of the slice: x: 2, y: 2, z: 4, core: 2. Of those that a mesh axis runs over, the one named last changes fastest.
Arguments:
- voltages: bfloat16 [1024, 2, 256, 512], P('freq', 'pol', 'beam'), may hold values from -6 to 6
- beam_weights: bfloat16 [256, 2, 1024, 512], P('freq', None, None, 'beam'), may hold values from -0.125 to 0.125
- delay_shifts: int32 [8, 256], replicated, may hold values from 0 to 255, as said below
Outputs:
- dedispersed: float32 [256, 2, 256, 256], P('freq', 'beam', 'pol')
Inputs may be any that keep to these rules, and one draw needn't show every extreme that they name: delay_shifts[s, d] lies between (d + 1) // 2 and d; only entries with d below 2 ** (s + 1) are read.
All inputs are finite; a program needn't handle non-finite values.
Results may differ from a plain program's by a relative error of at most 0.0006.
Values may be sent and summed in bfloat16 or wider, within the bound.
A program may use at most 256 MiB of HBM per device.

v0:
```python
import math

import jax
import jax.numpy as jnp
from jax import lax
from jax.sharding import PartitionSpec as P

F = 256


def swapped(shard, axis, bit):
    return lax.ppermute(shard, axis, [(i, i ^ 1 << bit) for i in range(lax.axis_size(axis))])


def fourier_table(length):
    index_row = jnp.arange(length, dtype=jnp.int32)
    product = index_row[:, None] * index_row[None, :] % length
    phase_angle = 2.0 * math.pi / length * product.astype(jnp.float32)
    norm_scale = 1.0 / math.sqrt(length)
    cosine = jnp.cos(phase_angle) * norm_scale
    sine_part = jnp.sin(phase_angle) * norm_scale
    real_rows = jnp.concatenate([cosine, sine_part], axis=1)
    imag_rows = jnp.concatenate([-sine_part, cosine], axis=1)
    return jnp.concatenate([real_rows, imag_rows], axis=0).astype(jnp.bfloat16)


def shift_rows(planes, amounts):
    length = planes.shape[-1]
    padded = jnp.concatenate([planes, jnp.zeros_like(planes)], axis=-1)
    return jax.vmap(
        lambda single_plane, amount: lax.dynamic_slice_in_dim(single_plane, amount, length, axis=1)
    )(padded, amounts)


def merge_level(planes, shift_row):
    first_half = planes[0::2]
    second_half = planes[1::2]
    widened = 2 * planes.shape[1]
    first_rep = jnp.repeat(first_half, 2, axis=1)
    second_rep = jnp.repeat(second_half, 2, axis=1)
    amounts = shift_row[:widened]
    shifted = jax.vmap(shift_rows, in_axes=(0, None))(second_rep, amounts)
    return first_rep + shifted


def contract(weights_part, volts_part):
    return jnp.einsum("cab,cas->cbs", weights_part, volts_part, preferred_element_type=jnp.float32)


def beam_power(real_weights, imag_weights, real_volts, imag_volts):
    real_beam = contract(real_weights, real_volts) - contract(imag_weights, imag_volts)
    imag_beam = contract(imag_weights, real_volts) + contract(real_weights, imag_volts)
    return real_beam * real_beam + imag_beam * imag_beam


def per_device(voltages, beam_weights, delay_shifts):
    freq_count = lax.axis_size("freq")
    beam_count = lax.axis_size("beam")
    rows_each = beam_weights.shape[0]
    fourier = fourier_table(F)
    channelized = lax.dot_general(
        fourier, voltages, (((1,), (3,)), ((), ())), preferred_element_type=jnp.float32
    )
    channelized = channelized.astype(jnp.bfloat16).reshape(
        2, F, voltages.shape[0], voltages.shape[2]
    )
    turned = lax.all_to_all(channelized, "freq", split_axis=1, concat_axis=2, tiled=True)
    piece = lax.all_gather(beam_weights, "beam", axis=3, tiled=True)
    powers = beam_power(piece[:, 0], piece[:, 1], turned[0], turned[1])
    grouped = powers.reshape(
        powers.shape[0], beam_count, powers.shape[1] // beam_count, powers.shape[2]
    )
    halved = lax.psum_scatter(
        grouped.astype(jnp.bfloat16), "pol", scatter_dimension=2, tiled=True
    ).astype(jnp.float32)
    regrouped = lax.all_to_all(
        halved.astype(jnp.bfloat16), "beam", split_axis=1, concat_axis=3, tiled=True
    ).astype(halved.dtype)
    summed = regrouped[:, 0]
    planes = summed[:, None]
    local_levels = rows_each.bit_length() - 1
    for level_index in range(local_levels):
        planes = merge_level(planes, delay_shifts[level_index])
    held_rows = planes[0]
    device = lax.axis_index("freq")
    position = jnp.zeros((), jnp.int32)
    half_rows = rows_each // 2
    for section_index in range(freq_count.bit_length() - 1):
        level_now = local_levels + section_index
        high_bit = device // 2**section_index % 2
        lower_side = high_bit == 0
        outgoing = jnp.where(lower_side, held_rows[half_rows:], held_rows[:half_rows])
        received = swapped(outgoing, "freq", section_index)
        first_rows = jnp.where(lower_side, held_rows[:half_rows], received)
        second_rows = jnp.where(lower_side, received, held_rows[half_rows:])
        position = 2 * position + high_bit
        amounts = lax.dynamic_slice_in_dim(delay_shifts[level_now], position * rows_each, rows_each)
        held_rows = jnp.repeat(first_rows, 2, axis=0) + shift_rows(
            jnp.repeat(second_rows, 2, axis=0), amounts
        )
    return (held_rows * (1.0 / (4 * F)))[:, None]


def solution(mesh):
    in_specs = (P("freq", "pol", "beam", None), P("freq", None, None, "beam"), P())
    out_specs = P("freq", "beam", "pol", None)
    return jax.shard_map(
        per_device, mesh=mesh, in_specs=in_specs, out_specs=out_specs, check_vma=False
    )
```

profile of v0, /device:TPU:0, one launch (start us, length us, event | category | flops | bytes accessed | tf_op | source)
XLA Modules:
  0.0 1511.0 jit_solution(10982855420951814088)
XLA Ops:
  6.5 22.9 %copy.25 = bf16[32,2,1024,256]{3,2,0,1:T(8,128)(2,1)} copy(bf16[32,2,1024,256]{3,2,1,0:T(8,128)(2,1)} %param.4) | data formatting | bytes 67108864 | tf_op args[1]
  31.6 24.3 %fusion.6 = bf16[512,128,128]{2,0,1:T(8,128)(2,1)} fusion(bf16[128,1,128,512]{3,2,1,0:T(8,128)(2,1)} %param.3, bf16[256,256]{1,0:T(8,128)(2,1)S(1)} %get-tuple-element.21, bf16[256,256]{1,0:T(8,128)(2,1)S(1)} %get-tuple-element.20, bf16[256,256]{1,0:T(8,128)(2,1)S(1)} %fusion.26), kind=kOutput, calls=%fused_computation.16 | convolution fusion | flops 8600420352 | bytes 33947648 | tf_op jit(solution)/shard_map/dot_general | solution.py:61
  55.9 23.5 %copy.23 = bf16[2,256,128,128]{3,0,2,1:T(2,128)(2,1)S(1)} copy(bf16[2,256,128,128]{3,1,0,2:T(8,128)(2,1)} %bitcast.158) | data formatting | bytes 33554432 | tf_op jit(solution)/shard_map/reshape | solution.py:64
  79.5 370.6 %all_to_all.24 = bf16[2,256,128,128]{3,0,2,1:T(2,128)(2,1)} all-to-all(bf16[2,256,128,128]{3,0,2,1:T(2,128)(2,1)S(1)} %copy.23), channel_id=1, replica_groups=mesh['freq'=8,'pol'=2,'beam'=2] {'freq'}, dimensions={1} | all-to-all | bytes 33554432 | tf_op jit(solution)/shard_map/all_to_all | solution.py:67
  450.1 27.9 %copy.24 = bf16[2,8,32,128,128]{3,1,4,2,0:T(8,128)(2,1)} copy(bf16[2,8,32,128,128]{4,0,3,2,1:T(2,128)(2,1)} %bitcast.152) | data formatting | bytes 33554432 | tf_op jit(solution)/shard_map/all_to_all | solution.py:67
  478.0 11.6 fusion.51
  489.6 13.3 squeeze.10
  502.9 13.3 squeeze.8
  516.2 284.0 %all-gather.2.cloned.1.call-done = bf16[32,2,1024,512]{3,2,0,1:T(8,128)(2,1)} async-done(((bf16[32,2,1024,256]{3,2,0,1:T(8,128)(2,1)}), bf16[32,2,1024,512]{3,2,0,1:T(8,128)(2,1)}) %all-gather.2.cloned.1.call-update) | async-done | bytes 67108880 | tf_op jit(solution)/shard_map/all_gather | solution.py:68
  800.2 19.4 %fusion.1 = f32[32,128,512]{2,1,0:T(8,128)} fusion(bf16[32,1024,128]{1,2,0:T(8,128)(2,1)} %squeeze.8, bf16[32,2,1024,512]{3,2,0,1:T(8,128)(2,1)} %all-gather.2.cloned.1.call-done), kind=kOutput, calls=%fused_computation.11 | convolution fusion | flops 4294967296 | bytes 50331648 | tf_op jit(solution)/shard_map/cab,cas->cbs/dot_general | solution.py:47
  819.6 19.4 %fusion.2 = f32[32,128,512]{2,1,0:T(8,128)} fusion(bf16[32,1024,128]{1,2,0:T(8,128)(2,1)} %squeeze.8, bf16[32,2,1024,512]{3,2,0,1:T(8,128)(2,1)} %all-gather.2.cloned.1.call-done), kind=kOutput, calls=%fused_computation.12 | convolution fusion | flops 4294967296 | bytes 50331648 | tf_op jit(solution)/shard_map/cab,cas->cbs/dot_general | solution.py:47
  839.0 19.4 %fusion = f32[32,128,512]{2,1,0:T(8,128)} fusion(bf16[32,1024,128]{1,2,0:T(8,128)(2,1)} %squeeze.10, bf16[32,2,1024,512]{3,2,0,1:T(8,128)(2,1)} %all-gather.2.cloned.1.call-done), kind=kOutput, calls=%fused_computation.10 | convolution fusion | flops 4294967296 | bytes 50331648 | tf_op jit(solution)/shard_map/cab,cas->cbs/dot_general | solution.py:47
  858.4 25.0 %fusion.9 = bf16[32,512,128]{1,2,0:T(8,128)(2,1)} fusion(f32[32,128,512]{2,1,0:T(8,128)} %fusion.2, f32[32,128,512]{2,1,0:T(8,128)} %fusion, f32[32,128,512]{2,1,0:T(8,128)} %fusion.1, bf16[32,1024,128]{1,2,0:T(8,128)(2,1)} %squeeze.10, bf16[32,2,1024,512]{3,2,0,1:T(8,128)(2,1)} %all-gather.2.cloned.1.call-done), kind=kOutput, calls=%fused_computation.19 | convolution fusion | flops 4307550208 | bytes 71303168 | tf_op jit(solution)/shard_map/cab,cas->cbs/dot_general | solution.py:47
  883.4 6.9 convert_element_type.49
  890.3 14.7 copy.37
  905.0 7.8 reshape.421
  913.5 11.5 reduce-scatter.4.cloned.1.call-done
  925.0 13.6 reshape.422
  938.6 4.0 copy.27
  942.6 3.8 all-to-all-start.1
  946.5 25.4 %all-to-all-done.1 = bf16[32,2,128,128]{2,3,0,1:T(8,128)(2,1)S(1)} async-done(((bf16[32,2,128,128]{2,3,0,1:T(8,128)(2,1)}), bf16[32,2,128,128]{2,3,0,1:T(8,128)(2,1)S(1)}, u32[]{:S(2)}, u32[]{:S(2)}) %all-to-all-start.1) | async-done | bytes 2097184 | tf_op jit(solution)/shard_map/all_to_all | solution.py:76
  975.7 4.2 concatenate.63
  980.0 6.2 gather_fusion
  986.2 4.6 add_bitcast_fusion
  990.8 11.5 slice.144
  1002.3 10.0 slice.143
  1014.4 4.2 concatenate.65
  1018.7 6.5 gather_fusion.1
  1025.1 4.5 bitcast_add_fusion.4
  1029.7 21.4 %slice.148 = f32[4,4,128,256]{2,0,3,1:T(4,128)} slice(f32[8,4,128,256]{2,0,3,1:T(8,128)} %bitcast_add_fusion.4), slice={[1:8:2], [0:4:1], [0:128:1], [0:256:1]} | slice | bytes 4194304 | tf_op jit(solution)/shard_map/slice | solution.py:37
  1051.0 19.6 %slice.147 = f32[4,4,128,256]{2,0,3,1:T(4,128)S(1)} slice(f32[8,4,128,256]{2,0,3,1:T(8,128)} %bitcast_add_fusion.4), slice={[0:8:2], [0:4:1], [0:128:1], [0:256:1]} | slice | bytes 4194304 | tf_op jit(solution)/shard_map/slice | solution.py:36
  1073.3 5.4 concatenate.67
  1078.6 9.0 gather_fusion.2
  1087.6 5.1 bitcast_add_fusion.3
  1092.7 39.5 %slice.152 = f32[2,8,128,256]{2,0,3,1:T(2,128)} slice(f32[4,8,128,256]{2,0,3,1:T(4,128)} %bitcast_add_fusion.3), slice={[1:4:2], [0:8:1], [0:128:1], [0:256:1]} | slice | bytes 4194304 | tf_op jit(solution)/shard_map/slice | solution.py:37
  1132.2 36.3 %slice.151 = f32[2,8,128,256]{2,0,3,1:T(2,128)S(1)} slice(f32[4,8,128,256]{2,0,3,1:T(4,128)} %bitcast_add_fusion.3), slice={[0:4:2], [0:8:1], [0:128:1], [0:256:1]} | slice | bytes 4194304 | tf_op jit(solution)/shard_map/slice | solution.py:36
  1170.8 3.3 broadcast_in_dim.69
  1174.1 9.6 concatenate.69
  1183.7 12.1 gather_fusion.3
  1195.9 4.0 bitcast_add_fusion.2
  1199.9 3.2 fusion.52
  1204.3 2.4 broadcast_in_dim.72
  1206.8 4.2 pad_bitcast_fusion
  1211.0 2.6 copy.34
  1213.7 10.3 gather_fusion.4
  1223.9 4.2 broadcast_in_dim.70
  1233.2 45.4 %collective-permute-done = f32[16,128,256]{1,0,2:T(8,128)} collective-permute-done((f32[16,128,256]{1,0,2:T(8,128)S(1)}, f32[16,128,256]{1,0,2:T(8,128)}, u32[]{:S(2)}, u32[]{:S(2)}) %collective-permute-start) | collective-permute-done | bytes 2097184 | tf_op jit(solution)/shard_map/ppermute | solution.py:12
  1278.6 4.7 fusion.13
  1283.4 2.4 broadcast_in_dim.75
  1285.8 4.2 concatenate.73
  1290.0 10.1 gather_fusion.5
  1300.2 4.2 broadcast_in_dim.74
  1309.5 44.7 %collective-permute-done.1 = f32[16,128,256]{1,0,2:T(8,128)} collective-permute-done((f32[16,128,256]{1,0,2:T(8,128)S(1)}, f32[16,128,256]{1,0,2:T(8,128)}, u32[]{:S(2)}, u32[]{:S(2)}) %collective-permute-start.1) | collective-permute-done | bytes 2097184 | tf_op jit(solution)/shard_map/ppermute | solution.py:12
  1354.2 4.7 slice_select_fusion.3
  1361.4 4.2 concatenate.75
  1365.6 10.1 gather_fusion.6
  1375.8 4.2 broadcast_in_dim.76
  1383.6 88.9 %collective-permute-done.2 = f32[16,128,256]{1,0,2:T(8,128)S(1)} collective-permute-done((f32[16,128,256]{1,0,2:T(8,128)S(1)}, f32[16,128,256]{1,0,2:T(8,128)S(1)}, u32[]{:S(2)}, u32[]{:S(2)}) %collective-permute-start.2) | collective-permute-done | bytes 2097184 | tf_op jit(solution)/shard_map/ppermute | solution.py:12
  1474.3 2.7 broadcast_in_dim.79
  1477.0 4.2 concatenate.77
  1481.2 10.1 gather_fusion.7
  1491.3 4.2 broadcast_in_dim.78
  1495.5 3.0 fusion.10
  1498.5 5.2 copy.36
  (49 shorter events, 33.0 us)
Async XLA Ops:
  6.5 793.7 %all-gather.2.cloned.1.call-start = ((), (), s32[]{:S(2)}) async-start(), calls=%async_computation.3 | async-start | bytes 100663296 | tf_op jit(solution)/shard_map/all_gather | solution.py:68
  29.4 895.5 %reduce-scatter.4.cloned.1.call-start = ((), (), s32[]{:S(2)}) async-start(), calls=%async_computation.4 | async-start | bytes 6291456
  912.8 0.7 copy-start.6
  942.6 29.4 %all-to-all-start.1 = ((bf16[32,2,128,128]{2,3,0,1:T(8,128)(2,1)}), bf16[32,2,128,128]{2,3,0,1:T(8,128)(2,1)S(1)}, u32[]{:S(2)}, u32[]{:S(2)}) async-start(bf16[32,2,128,128]{2,3,0,1:T(8,128)(2,1)} %copy.27), calls=%async_computation.1 | async-start | bytes 4194304 | tf_op jit(solution)/shard_map/all_to_all | solution.py:76
  1223.9 4.2 copy-start.5
  1229.2 2.0 copy-start.1
  1231.5 47.2 %collective-permute-start = (f32[16,128,256]{1,0,2:T(8,128)S(1)}, f32[16,128,256]{1,0,2:T(8,128)}, u32[]{:S(2)}, u32[]{:S(2)}) collective-permute-start(f32[16,128,256]{1,0,2:T(8,128)S(1)} %fusion.12), channel_id=1, source_target_pairs={{0,4},{4,0},{8,12},{12,8},{16,20},{20,16},{24,28},{28,24},{1,5},{5... | collective-permute-start | bytes 6291464 | tf_op jit(solution)/shard_map/ppermute | solution.py:12
  1300.2 4.2 copy-start.2
  1305.6 2.0 copy-start
  1307.9 46.3 %collective-permute-start.1 = (f32[16,128,256]{1,0,2:T(8,128)S(1)}, f32[16,128,256]{1,0,2:T(8,128)}, u32[]{:S(2)}, u32[]{:S(2)}) collective-permute-start(f32[16,128,256]{1,0,2:T(8,128)S(1)} %slice_select_fusion.4), channel_id=1, source_target_pairs={{0,8},{4,12},{8,0},{12,4},{16,24},{20,28},{24,16},{28,20},{1,9},{5... | collective-permute-start | bytes 6291464 | tf_op jit(solution)/shard_map/ppermute | solution.py:12
  1375.8 4.2 copy-start.3
  1381.3 91.2 %collective-permute-start.2 = (f32[16,128,256]{1,0,2:T(8,128)S(1)}, f32[16,128,256]{1,0,2:T(8,128)S(1)}, u32[]{:S(2)}, u32[]{:S(2)}) collective-permute-start(f32[16,128,256]{1,0,2:T(8,128)S(1)} %slice_select_fusion.1), channel_id=1, source_target_pairs={{0,16},{4,20},{8,24},{12,28},{16,0},{20,4},{24,8},{28,12},{1,17},{... | collective-permute-start | bytes 6291464 | tf_op jit(solution)/shard_map/ppermute | solution.py:12
  1491.3 4.2 copy-start.4
Sparse Core Ops, SparseCore 0:
  29.5 770.6 all-gather.1
  912.9 12.0 reduce-scatter.3
where the time goes:
time: 1520 us; the launch traced here: 1510 us
  waiting for transfers between devices  500 us (33%)
  local copies, waits for them, and re-layouts  470 us (31%)
  blocking collectives  371 us (24%)
  matrix products  108 us (7%)
  other arithmetic  39.4 us (3%)
    all_to_all x1, blocking collectives, per_device(): lax.all_to_all(channelized, 'freq', split_axis=1, concat_axis=2, tiled=True)  371 us
    all_gather x1, waiting for transfers between devices, per_device(): piece = lax.all_gather(beam_weights, 'beam', axis=3, tiled=True)  284 us
    ppermute x3, waiting for transfers between devices, swapped(): lax.ppermute(shard, axis, [(i, i ^ 1 << bit) for i in range(lax.axis_size...  179 us
    slice x9, local copies, waits for them, and re-layouts, merge_level(): second_half = planes[1::2]  84 us
    dot_general x4, matrix products, contract(): jnp.einsum('cab,cas->cbs', weights_part, volts_part, preferred_element_ty...  83.2 us
    gather x8, local copies, waits for them, and re-layouts, shift_rows(): lax.dynamic_slice_in_dim(single_plane, amount, length, axis=1)  74.4 us
    slice x6, local copies, waits for them, and re-layouts, merge_level(): first_half = planes[0::2]  70.1 us
    unnamed x18, local copies, waits for them, and re-layouts  63.6 us
  transfers between devices with their start and end apart: 6, of which 6 were waited for; matrix products, arithmetic and copies ran while one was open for 8% of the time, Pallas kernels for 0%

commit v1 on v0

v1 whole, which is shorter than its diff:
```python
import functools
import math

import jax
import jax.numpy as jnp
from jax import lax
from jax.experimental import pallas as pl
from jax.experimental.pallas import tpu as pltpu
from jax.sharding import PartitionSpec as P

F = 256
PIECES = 2


def swapped(shard, axis, bit):
    return lax.ppermute(shard, axis, [(i, i ^ 1 << bit) for i in range(lax.axis_size(axis))])


def fourier_table(length):
    index_row = jnp.arange(length, dtype=jnp.int32)
    product = index_row[:, None] * index_row[None, :] % length
    phase_angle = 2.0 * math.pi / length * product.astype(jnp.float32)
    norm_scale = 1.0 / math.sqrt(length)
    cosine = jnp.cos(phase_angle) * norm_scale
    sine_part = jnp.sin(phase_angle) * norm_scale
    real_rows = jnp.concatenate([cosine, sine_part], axis=1)
    imag_rows = jnp.concatenate([-sine_part, cosine], axis=1)
    return jnp.concatenate([real_rows, imag_rows], axis=0).astype(jnp.bfloat16)


def antenna_rows(ref, part):
    block = ref[:, part, 0]
    sources, antennas, length = block.shape
    if antennas % 16 == 0:
        return block.reshape(sources * antennas, length)
    wide = block.astype(jnp.float32).reshape(sources * antennas, length)
    return wide.astype(block.dtype)


def over_antennas(volts, weights):
    return lax.dot_general(
        volts, weights, (((0,), (0,)), ((), ())), preferred_element_type=jnp.float32
    )


def power_kernel(own_volts, other_volts, own_weights, other_weights, own_power, other_power):
    real_volts = jnp.concatenate([antenna_rows(own_volts, 0), antenna_rows(other_volts, 0)], axis=1)
    imag_volts = jnp.concatenate([antenna_rows(own_volts, 1), antenna_rows(other_volts, 1)], axis=1)
    real_weights = jnp.concatenate([own_weights[0, 0], other_weights[0, 0]], axis=1)
    imag_weights = jnp.concatenate([own_weights[0, 1], other_weights[0, 1]], axis=1)
    real_beam = over_antennas(real_volts, real_weights) - over_antennas(imag_volts, imag_weights)
    imag_beam = over_antennas(real_volts, imag_weights) + over_antennas(imag_volts, real_weights)
    both = real_beam * real_beam + imag_beam * imag_beam
    half = both.shape[0] // 2
    power = both[:half] + both[half:]
    beams = own_weights.shape[3]
    own_power[0] = power[:, :beams]
    other_power[0] = power[:, beams:].astype(other_power.dtype)


def beam_power(own_volts, other_volts, own_weights, other_weights, offset):
    sources, _, channels, antennas, length = own_volts.shape
    beams = own_weights.shape[3]
    volt_spec = pl.BlockSpec((sources, 2, 1, antennas, length), lambda c: (0, 0, c, 0, 0))
    weight_spec = pl.BlockSpec(
        (1, 2, own_weights.shape[2], beams), lambda c: (c + offset, 0, 0, 0)
    )
    power_spec = pl.BlockSpec((1, length, beams), lambda c: (c, 0, 0))
    macs = channels * sources * antennas * length * beams * 16
    return pl.pallas_call(
        power_kernel,
        grid=(channels,),
        in_specs=[volt_spec, volt_spec, weight_spec, weight_spec],
        out_specs=[power_spec, power_spec],
        out_shape=[
            jax.ShapeDtypeStruct((channels, length, beams), jnp.float32),
            jax.ShapeDtypeStruct((channels, length, beams), jnp.bfloat16),
        ],
        compiler_params=pltpu.CompilerParams(vmem_limit_bytes=40 * 2**20),
        cost_estimate=pl.CostEstimate(
            flops=2 * macs, bytes_accessed=2 * own_volts.size * 4, transcendentals=0
        ),
    )(own_volts, other_volts, own_weights, other_weights)


def emit_rows(make_row, half_rows, high, keep_ref, send_ref):
    def body(row, carry):
        keep_ref[row] = make_row(high * half_rows + row)
        send_ref[row] = make_row((1 - high) * half_rows + row)
        return carry

    lax.fori_loop(0, half_rows, body, 0)


def tree_kernel(levels, info, shifts, own, other, keep_ref, send_ref, ping, pong):
    channels, part, _ = own.shape
    length = 2 * part
    side = info[0]
    device = info[1]
    ping[:, length:] = jnp.zeros_like(ping[:, length:])
    pong[:, length:] = jnp.zeros_like(pong[:, length:])

    def fill(row, carry):
        ping[row, pl.ds(pl.multiple_of(side * part, 8), part)] = own[row]
        ping[row, pl.ds(pl.multiple_of((1 - side) * part, 8), part)] = other[row].astype(jnp.float32)
        return carry

    lax.fori_loop(0, channels, fill, 0)
    source, target = ping, pong
    for level in range(levels):

        def make_row(row, source=source, level=level):
            group = row >> (level + 1)
            delay = row & ((2 << level) - 1)
            first = (2 * group << level) + (delay >> 1)
            second = first + (1 << level)
            return source[first, :length] + source[second, pl.ds(shifts[level, delay], length)]

        if level < levels - 1:

            def body(row, carry, make_row=make_row, target=target):
                target[row, :length] = make_row(row)
                return carry

            lax.fori_loop(0, channels, body, 0)
            source, target = target, source
        else:
            emit_rows(make_row, channels // 2, device & 1, keep_ref, send_ref)


def section_kernel(section, sections, level, scale, info, shifts, kept, received, *rest):
    outs, held = rest[:-1], rest[-1]
    half_rows, length, _ = kept.shape
    rows = 2 * half_rows
    device = info[1]
    high = (device >> section) & 1
    position = 0
    for bit in range(section + 1):
        position = 2 * position + ((device >> bit) & 1)
    held[:, :, length:] = jnp.zeros_like(held[:, :, length:])

    def fill(row, carry):
        held[high, row, :length] = kept[row]
        held[1 - high, row, :length] = received[row]
        return carry

    lax.fori_loop(0, half_rows, fill, 0)

    def make_row(row):
        amount = shifts[level, position * rows + row]
        return held[0, row >> 1, :length] + held[1, row >> 1, pl.ds(amount, length)]

    if section + 1 < sections:
        emit_rows(make_row, half_rows, (device >> (section + 1)) & 1, *outs)
    else:

        def body(row, carry):
            outs[0][row] = jnp.transpose(make_row(row) * scale)
            return carry

        lax.fori_loop(0, rows, body, 0)


SMEM_SPEC = pl.BlockSpec(memory_space=pltpu.SMEM)
VMEM_SPEC = pl.BlockSpec(memory_space=pltpu.VMEM)


def per_device(voltages, beam_weights, delay_shifts):
    sources = lax.axis_size("freq")
    rows_each = beam_weights.shape[0]
    beams = beam_weights.shape[3] // lax.axis_size("pol")
    antennas, _, spectra, samples = voltages.shape
    device = lax.axis_index("freq")
    side = lax.axis_index("beam")
    core = lax.axis_index("pol")
    info = jnp.stack([side, device]).astype(jnp.int32)

    own_weights = lax.dynamic_slice_in_dim(beam_weights, core * beams, beams, axis=3)
    other_weights = swapped(own_weights, "beam", 0)

    pieces = PIECES if rows_each % PIECES == 0 else 1
    each = rows_each // pieces
    table = fourier_table(F).reshape(2, sources, rows_each, samples).transpose(1, 0, 2, 3)
    own_parts, other_parts = [], []
    turned_parts = []
    for piece in range(pieces):
        rows = table[:, :, piece * each : (piece + 1) * each].reshape(-1, samples)
        channelized = lax.dot_general(
            rows, voltages[:, 0], (((1,), (2,)), ((), ())), preferred_element_type=jnp.float32
        )
        channelized = channelized.astype(jnp.bfloat16).reshape(
            sources, 2, each, antennas, spectra
        )
        turned = lax.all_to_all(channelized, "freq", split_axis=0, concat_axis=0)
        turned_parts.append((turned, swapped(turned, "pol", 0)))
    for piece, (turned, other_turned) in enumerate(turned_parts):
        own, other = beam_power(turned, other_turned, own_weights, other_weights, piece * each)
        own_parts.append(own)
        other_parts.append(swapped(other, "beam", 0))
    own_power = jnp.concatenate(own_parts, axis=0)
    other_power = jnp.concatenate(other_parts, axis=0)

    length = 2 * spectra
    levels = rows_each.bit_length() - 1
    sections = sources.bit_length() - 1
    half = jax.ShapeDtypeStruct((rows_each // 2, length, beams), jnp.float32)
    kept, sent = pl.pallas_call(
        functools.partial(tree_kernel, levels),
        in_specs=[SMEM_SPEC, SMEM_SPEC, VMEM_SPEC, VMEM_SPEC],
        out_specs=[VMEM_SPEC, VMEM_SPEC],
        out_shape=[half, half],
        scratch_shapes=[pltpu.VMEM((rows_each, 2 * length, beams), jnp.float32)] * 2,
        compiler_params=pltpu.CompilerParams(vmem_limit_bytes=40 * 2**20),
    )(info, delay_shifts, own_power, other_power)
    for section in range(sections):
        received = swapped(sent, "freq", section)
        last = section + 1 == sections
        shape = [jax.ShapeDtypeStruct((rows_each, beams, length), jnp.float32)] if last else [half] * 2
        result = pl.pallas_call(
            functools.partial(
                section_kernel, section, sections, levels + section, 1.0 / (4 * F)
            ),
            in_specs=[SMEM_SPEC, SMEM_SPEC, VMEM_SPEC, VMEM_SPEC],
            out_specs=[VMEM_SPEC] * len(shape),
            out_shape=shape,
            scratch_shapes=[pltpu.VMEM((2, rows_each // 2, 2 * length, beams), jnp.float32)],
            compiler_params=pltpu.CompilerParams(vmem_limit_bytes=40 * 2**20),
        )(info, delay_shifts, kept, received)
        if last:
            return result[0][:, None]
        kept, sent = result


def solution(mesh):
    in_specs = (P("freq", "pol", "beam", None), P("freq", None, None, "beam"), P())
    out_specs = P("freq", "beam", "pol", None)
    return jax.shard_map(
        per_device, mesh=mesh, in_specs=in_specs, out_specs=out_specs, check_vma=False
    )
```

time: 1520 us -> 846 us (0.56)
  local copies, waits for them, and re-layouts: 470 us -> 41.1 us
  blocking collectives: 371 us -> 0 us
  waiting for transfers between devices: 500 us -> 704 us
  matrix products: 108 us -> 20.3 us
  Pallas kernels: 0 us -> 54.8 us
  other arithmetic: 39.4 us -> 3.64 us
    all_to_all x1 -> x0, blocking collectives: 371 us -> none  [per_device(): lax.all_to_all(channelized, 'freq', split_axis=1, concat_axis=2, tiled=True)]
    all_to_all x1 -> x2, waiting for transfers between devices: 25.4 us -> 328 us  [per_device(): turned = lax.all_to_all(channelized, 'freq', split_axis=0, concat_axis=0)]
    all_gather x1 -> x0, waiting for transfers between devices: 284 us -> none  [per_device(): piece = lax.all_gather(beam_weights, 'beam', axis=3, tiled=True)]
    ppermute x3 -> x8, waiting for transfers between devices: 179 us -> 376 us  [swapped(): lax.ppermute(shard, axis, [(i, i ^ 1 << bit) for i in range(lax.axis_size...]
    slice x17 -> x3, local copies, waits for them, and re-layouts: 166 us -> 0.07 us  [per_device(): rows = table[:, :, piece * each:(piece + 1) * each].reshape(-1, samples)]
    dot_general x5 -> x2, matrix products: 108 us -> 20.3 us  [per_device(): lax.dot_general(rows, voltages[:, 0], (((1,), (2,)), ((), ())), preferred...]
    gather x8 -> x0, local copies, waits for them, and re-layouts: 74.4 us -> none  [shift_rows(): lax.dynamic_slice_in_dim(single_plane, amount, length, axis=1)]
    unnamed x18 -> x4, local copies, waits for them, and re-layouts: 63.6 us -> 3.23 us
  transfers between devices with their start and end apart: 6 -> 10, of which waited for: 6 -> 7; matrix products, arithmetic and copies ran while one was open for 8% -> 4% of each run, Pallas kernels for 0% -> 5%
where the time goes in v1:
time: 846 us; the launch traced here: 845 us
  waiting for transfers between devices  704 us (83%)
  Pallas kernels  54.8 us (6%)
  local copies, waits for them, and re-layouts  41.1 us (5%)
  starting transfers between devices  20.8 us (2%)
  matrix products  20.3 us (2%)
    ppermute x8, waiting for transfers between devices, swapped(): lax.ppermute(shard, axis, [(i, i ^ 1 << bit) for i in range(lax.axis_size...  376 us
    all_to_all x2, waiting for transfers between devices, per_device(): turned = lax.all_to_all(channelized, 'freq', split_axis=0, concat_axis=0)  328 us
    pallas_call x2, Pallas kernels, beam_power(): pl.pallas_call(power_kernel, grid=(channels,), in_specs=[volt_spec, volt_...  39.8 us
    convert_element_type x2, local copies, waits for them, and re-layouts, per_device(): channelized.astype(jnp.bfloat16)  24 us
    dot_general x2, matrix products, per_device(): lax.dot_general(rows, voltages[:, 0], (((1,), (2,)), ((), ())), preferred...  20.3 us
  transfers between devices with their start and end apart: 10, of which 7 were waited for; matrix products, arithmetic and copies ran while one was open for 4% of the time, Pallas kernels for 5%

profile of v1, /device:TPU:0, one launch (start us, length us, event | category | flops | bytes accessed | tf_op | source)
XLA Modules:
  0.0 844.8 jit_solution(2706271933905791452)
XLA Ops:
  0.0 1.1 negate_convert_fusion
  1.1 1.0 fusion.16
  2.2 10.1 %fusion.4 = bf16[256,128,128]{2,0,1:T(8,128)(2,1)} fusion(bf16[256,512,1]{1,0,2:T(8,128)(2,1)S(1)} %bitcast.30, bf16[128,1,128,512]{3,2,1,0:T(8,128)(2,1)} %param.3), kind=kOutput, calls=%fused_computation.4 | convolution fusion | flops 4299161600 | bytes 25427968 | tf_op jit(solution)/shard_map/dot_general | solution.py:188
  12.4 12.0 %copy.8 = bf16[256,128,128]{2,1,0:T(8,128)(2,1)} copy(bf16[256,128,128]{2,0,1:T(8,128)(2,1)} %fusion.4) | data formatting | bytes 16777216 | tf_op jit(solution)/shard_map/convert_element_type | solution.py:191
  24.4 7.3 all-to-all-start
  31.7 10.1 %fusion.7 = bf16[256,128,128]{2,0,1:T(8,128)(2,1)} fusion(bf16[256,512,1]{1,0,2:T(8,128)(2,1)S(1)} %bitcast.31, bf16[128,1,128,512]{3,2,1,0:T(8,128)(2,1)} %param.3), kind=kOutput, calls=%fused_computation.5 | convolution fusion | flops 4299161600 | bytes 25427968 | tf_op jit(solution)/shard_map/dot_general | solution.py:188
  41.8 12.0 %copy.10 = bf16[256,128,128]{2,1,0:T(8,128)(2,1)} copy(bf16[256,128,128]{2,0,1:T(8,128)(2,1)} %fusion.7) | data formatting | bytes 16777216 | tf_op jit(solution)/shard_map/convert_element_type | solution.py:191
  53.8 161.0 %all-to-all-done.own_volts = bf16[8,2,16,128,128]{4,3,2,1,0:T(8,128)(2,1)} async-done(((bf16[8,2,16,128,128]{4,3,2,1,0:T(8,128)(2,1)}), bf16[8,2,16,128,128]{4,3,2,1,0:T(8,128)(2,1)}, u32[]{:S(2)}, u32[]{:S(2)}) %all-to-all-start) | async-done | bytes 8388640 | tf_op jit(solution)/shard_map/all_to_all | solution.py:194
  214.8 5.2 all-to-all-start.1
  220.0 13.8 %constant_dynamic-slice_fusion.own_weights = bf16[32,2,1024,128]{3,2,1,0:T(8,128)(2,1)} fusion(bf16[32,2,1024,256]{3,2,1,0:T(8,128)(2,1)} %param.4, s32[]{:T(128)S(6)} %select_n.17), kind=kLoop, calls=%fused_computation.23 | loop fusion | bytes 33554436 | tf_op jit(solution)/shard_map/dynamic_slice | solution.py:178
  233.8 1.5 collective-permute-start.1
  235.3 0.0 collective-permute-start
  235.3 166.7 %all-to-all-done.1.own_volts = bf16[8,2,16,128,128]{4,3,2,1,0:T(8,128)(2,1)} async-done(((bf16[8,2,16,128,128]{4,3,2,1,0:T(8,128)(2,1)}), bf16[8,2,16,128,128]{4,3,2,1,0:T(8,128)(2,1)}, u32[]{:S(2)}, u32[]{:S(2)}) %all-to-all-start.1) | async-done | bytes 8388640 | tf_op jit(solution)/shard_map/all_to_all | solution.py:194
  402.0 0.0 collective-permute-start.2
  402.0 192.9 %collective-permute-done.1.other_weights = bf16[32,2,1024,128]{3,2,1,0:T(8,128)(2,1)} collective-permute-done((bf16[32,2,1024,128]{3,2,1,0:T(8,128)(2,1)}, bf16[32,2,1024,128]{3,2,1,0:T(8,128)(2,1)}, u32[]{:S(2)}, u32[]{:S(2)}) %collective-permute-start.1) | collective-permute-done | bytes 16777248 | tf_op jit(solution)/shard_map/ppermute | solution.py:16
  595.0 0.0 collective-permute-done.other_volts
  595.0 19.9 %shard_map.37 = (f32[16,128,128]{2,1,0:T(8,128)S(1)}, bf16[16,128,128]{2,1,0:T(8,128)(2,1)S(1)}) custom-call(bf16[8,2,16,128,128]{4,3,2,1,0:T(8,128)(2,1)} %all-to-all-done.own_volts, bf16[8,2,16,128,128]{4,3,2,1,0:T(8,128)(2,1)} %collective-permute-done.other_volts, bf16[32,2,1024,128]{3,2,1,0:T(8,128)(2,1)} %constant_dynamic-slice_fusion.own_weights, ...), custom_call_target="tpu_custom_call" | custom-call | flops 8589934592 | bytes 33554432 | tf_op jit(solution)/shard_map/pallas_call | solution.py:70
  614.9 0.0 copy-start
  614.9 1.6 collective-permute-start.3
  616.5 0.0 collective-permute-done.2.other_volts
  616.5 0.0 copy-start.1
  616.5 3.2 copy-done.1
  619.7 19.9 %shard_map.38 = (f32[16,128,128]{2,1,0:T(8,128)S(1)}, bf16[16,128,128]{2,1,0:T(8,128)(2,1)S(1)}) custom-call(bf16[8,2,16,128,128]{4,3,2,1,0:T(8,128)(2,1)} %all-to-all-done.1.own_volts, bf16[8,2,16,128,128]{4,3,2,1,0:T(8,128)(2,1)} %copy-done.1, bf16[32,2,1024,128]{3,2,1,0:T(8,128)(2,1)} %constant_dynamic-slice_fusion.own_weights, ...), custom_call_target="tpu_custom_call" | custom-call | flops 8589934592 | bytes 33554432 | tf_op jit(solution)/shard_map/pallas_call | solution.py:70
  639.6 0.6 collective-permute-start.4
  640.2 0.1 pad_add_fusion.info
  640.3 0.1 pad_maximum_fusion.own
  640.4 0.0 collective-permute-done.3
  640.4 10.8 %collective-permute-done.4 = bf16[16,128,128]{2,1,0:T(8,128)(2,1)} collective-permute-done((bf16[16,128,128]{2,1,0:T(8,128)(2,1)S(1)}, bf16[16,128,128]{2,1,0:T(8,128)(2,1)}, u32[]{:S(2)}, u32[]{:S(2)}) %collective-permute-start.4) | collective-permute-done | bytes 524320 | tf_op jit(solution)/shard_map/ppermute | solution.py:16
  651.2 1.3 pad_maximum_fusion.1.other
  652.5 0.0 copy-done
  652.5 4.6 shard_map.39
  657.1 2.0 collective-permute-start.5
  659.2 42.7 %collective-permute-done.5.received = f32[16,256,128]{2,1,0:T(8,128)S(1)} collective-permute-done((f32[16,256,128]{2,1,0:T(8,128)S(1)}, f32[16,256,128]{2,1,0:T(8,128)S(1)}, u32[]{:S(2)}, u32[]{:S(2)}) %collective-permute-start.5) | collective-permute-done | bytes 2097184 | tf_op jit(solution)/shard_map/ppermute | solution.py:16
  701.9 1.8 shard_map.40
  703.7 0.5 collective-permute-start.6
  704.2 43.4 %collective-permute-done.6.received = f32[16,256,128]{2,1,0:T(8,128)S(1)} collective-permute-done((f32[16,256,128]{2,1,0:T(8,128)S(1)}, f32[16,256,128]{2,1,0:T(8,128)S(1)}, u32[]{:S(2)}, u32[]{:S(2)}) %collective-permute-start.6) | collective-permute-done | bytes 2097184 | tf_op jit(solution)/shard_map/ppermute | solution.py:16
  747.5 1.8 shard_map.41
  749.4 2.1 collective-permute-start.7
  751.5 86.6 %collective-permute-done.7.received = f32[16,256,128]{2,1,0:T(8,128)S(1)} collective-permute-done((f32[16,256,128]{2,1,0:T(8,128)S(1)}, f32[16,256,128]{2,1,0:T(8,128)S(1)}, u32[]{:S(2)}, u32[]{:S(2)}) %collective-permute-start.7) | collective-permute-done | bytes 2097184 | tf_op jit(solution)/shard_map/ppermute | solution.py:16
  838.0 6.8 shard_map.42
  (4 shorter events, 0.1 us)
Async XLA Ops:
  24.4 190.5 %all-to-all-start = ((bf16[8,2,16,128,128]{4,3,2,1,0:T(8,128)(2,1)}), bf16[8,2,16,128,128]{4,3,2,1,0:T(8,128)(2,1)}, u32[]{:S(2)}, u32[]{:S(2)}) async-start(bf16[8,2,16,128,128]{4,3,2,1,0:T(8,128)(2,1)} %bitcast.28), calls=%async_computation | async-start | bytes 16777216 | tf_op jit(solution)/shard_map/all_to_all | solution.py:194
  214.8 187.2 %all-to-all-start.1 = ((bf16[8,2,16,128,128]{4,3,2,1,0:T(8,128)(2,1)}), bf16[8,2,16,128,128]{4,3,2,1,0:T(8,128)(2,1)}, u32[]{:S(2)}, u32[]{:S(2)}) async-start(bf16[8,2,16,128,128]{4,3,2,1,0:T(8,128)(2,1)} %bitcast.27), calls=%async_computation.1 | async-start | bytes 16777216 | tf_op jit(solution)/shard_map/all_to_all | solution.py:194
  233.8 361.2 %collective-permute-start.1 = (bf16[32,2,1024,128]{3,2,1,0:T(8,128)(2,1)}, bf16[32,2,1024,128]{3,2,1,0:T(8,128)(2,1)}, u32[]{:S(2)}, u32[]{:S(2)}) collective-permute-start(bf16[32,2,1024,128]{3,2,1,0:T(8,128)(2,1)} %constant_dynamic-slice_fusion.own_weights), channel_id=1, source_target_pairs={{0,1},{1,0},{2,3},{3,2},{4,5},{5,4},{6,7},{7,6},{8,9},{9,8},{10,11... | collective-permute-start | bytes 50331656 | tf_op jit(solution)/shard_map/ppermute | solution.py:16
  235.3 359.7 %collective-permute-start = (bf16[8,2,16,128,128]{4,3,2,1,0:T(8,128)(2,1)}, bf16[8,2,16,128,128]{4,3,2,1,0:T(8,128)(2,1)}, u32[]{:S(2)}, u32[]{:S(2)}) collective-permute-start(bf16[8,2,16,128,128]{4,3,2,1,0:T(8,128)(2,1)} %all-to-all-done.own_volts), channel_id=1, source_target_pairs={{0,2},{2,0},{1,3},{3,1},{4,6},{6,4},{5,7},{7,5},{8,10},{10,8},{9,1... | collective-permute-start | bytes 25165832 | tf_op jit(solution)/shard_map/ppermute | solution.py:16
  402.0 214.4 %collective-permute-start.2 = (bf16[8,2,16,128,128]{4,3,2,1,0:T(8,128)(2,1)}, bf16[8,2,16,128,128]{4,3,2,1,0:T(8,128)(2,1)S(1)}, u32[]{:S(2)}, u32[]{:S(2)}) collective-permute-start(bf16[8,2,16,128,128]{4,3,2,1,0:T(8,128)(2,1)} %all-to-all-done.1.own_volts), channel_id=1, source_target_pairs={{0,2},{2,0},{1,3},{3,1},{4,6},{6,4},{5,7},{7,5},{8,10},{10,8},{9,1... | collective-permute-start | bytes 25165832 | tf_op jit(solution)/shard_map/ppermute | solution.py:16
  614.9 37.7 %copy-start = (s32[8,256]{1,0:T(8,128)S(1)}, s32[8,256]{1,0:T(8,128)}, u32[]{:S(2)}) copy-start(s32[8,256]{1,0:T(8,128)} %shifts.7) | copy-start | bytes 24580
  614.9 25.5 %collective-permute-start.3 = (bf16[16,128,128]{2,1,0:T(8,128)(2,1)S(1)}, bf16[16,128,128]{2,1,0:T(8,128)(2,1)}, u32[]{:S(2)}, u32[]{:S(2)}) collective-permute-start(bf16[16,128,128]{2,1,0:T(8,128)(2,1)S(1)} %get-tuple-element.17), channel_id=1, source_target_pairs={{0,1},{1,0},{2,3},{3,2},{4,5},{5,4},{6,7},{7,6},{8,9},{9,8},{10,11... | collective-permute-start | bytes 1572872 | tf_op jit(solution)/shard_map/ppermute | solution.py:16
  616.5 3.2 copy-start.1
  639.6 11.6 %collective-permute-start.4 = (bf16[16,128,128]{2,1,0:T(8,128)(2,1)S(1)}, bf16[16,128,128]{2,1,0:T(8,128)(2,1)}, u32[]{:S(2)}, u32[]{:S(2)}) collective-permute-start(bf16[16,128,128]{2,1,0:T(8,128)(2,1)S(1)} %get-tuple-element.18), channel_id=1, source_target_pairs={{0,1},{1,0},{2,3},{3,2},{4,5},{5,4},{6,7},{7,6},{8,9},{9,8},{10,11... | collective-permute-start | bytes 1572872 | tf_op jit(solution)/shard_map/ppermute | solution.py:16
  657.1 44.7 %collective-permute-start.5 = (f32[16,256,128]{2,1,0:T(8,128)S(1)}, f32[16,256,128]{2,1,0:T(8,128)S(1)}, u32[]{:S(2)}, u32[]{:S(2)}) collective-permute-start(f32[16,256,128]{2,1,0:T(8,128)S(1)} %get-tuple-element.20), channel_id=1, source_target_pairs={{0,4},{4,0},{8,12},{12,8},{16,20},{20,16},{24,28},{28,24},{1,5},{5... | collective-permute-start | bytes 6291464 | tf_op jit(solution)/shard_map/ppermute | solution.py:16
  703.7 43.9 %collective-permute-start.6 = (f32[16,256,128]{2,1,0:T(8,128)S(1)}, f32[16,256,128]{2,1,0:T(8,128)S(1)}, u32[]{:S(2)}, u32[]{:S(2)}) collective-permute-start(f32[16,256,128]{2,1,0:T(8,128)S(1)} %get-tuple-element.22), channel_id=1, source_target_pairs={{0,8},{4,12},{8,0},{12,4},{16,24},{20,28},{24,16},{28,20},{1,9},{5... | collective-permute-start | bytes 6291464 | tf_op jit(solution)/shard_map/ppermute | solution.py:16
  749.4 88.7 %collective-permute-start.7 = (f32[16,256,128]{2,1,0:T(8,128)S(1)}, f32[16,256,128]{2,1,0:T(8,128)S(1)}, u32[]{:S(2)}, u32[]{:S(2)}) collective-permute-start(f32[16,256,128]{2,1,0:T(8,128)S(1)} %get-tuple-element.24), channel_id=1, source_target_pairs={{0,16},{4,20},{8,24},{12,28},{16,0},{20,4},{24,8},{28,12},{1,17},{... | collective-permute-start | bytes 6291464 | tf_op jit(solution)/shard_map/ppermute | solution.py:16
